TPU v7x, 128 devices: a whole 4x4x4 slice. The times are simulated.
128 devices in a mesh: exa: 8 (over z, core), exb: 16 (over x, y).
Axes of the slice: x: 4, y: 4, z: 4, core: 2. Of those that a mesh axis runs over, the one named last changes fastest.
Arguments:
- features: float32 [1048576, 128], P(('exa', 'exb')), may hold values from -6 to 6
- sign_bits: int32 [1048576], P(('exa', 'exb')), may hold values from 0 to 1
- sample_device: int32 [65536, 1], replicated, may hold values from 0 to 127; in each aligned block of 512 rows (0 to 511, 512 to 1023, ...) at most 8 rows name the same one
- sample_offset: int32 [65536], replicated, may hold values from 0 to 8191, as said below
Outputs:
- q_rows: float32 [65536, 128], P(('exa', 'exb'))
- upper_factor: float32 [128, 128], replicated
Inputs may be any that keep to these rules, and one draw needn't show every extreme that they name: `sample_device`: within each aligned block of 512 rows no value appears more than 8 times. `sample_offset`: within each aligned block of 512 rows, at most 8 values fall into any one range of 64 consecutive offsets that starts at a multiple of 64, and in every block some range holds exactly 8.
All inputs are finite; a program needn't handle non-finite values.
Results may differ from a plain program's by a relative error of at most 0.000071.
Values sent between devices are 32-bit elements; how exact they have to be, the bound alone decides.
A program may use at most 64 MiB of HBM per device.

v0:
```python
import math

import jax
import jax.numpy as jnp
from jax import lax
from jax.sharding import PartitionSpec as P


def over_pieces(x, axis):
    blocks = lax.all_gather(x, axis)
    return blocks.sum(axis=0)


def hadamard_table(order_size):
    index = jnp.arange(order_size, dtype=jnp.int32)
    common = index[:, None] & index[None, :]
    parity = jnp.zeros((order_size, order_size), jnp.int32)
    for bit_pos in range(max(order_size.bit_length(), 1)):
        parity = parity + (common >> bit_pos & 1)
    return (1 - 2 * (parity % 2)).astype(jnp.float32)


def cholesky_upper(gram):
    width = gram.shape[0]
    columns = jnp.arange(width, dtype=jnp.int32)

    def cholesky_one_row(step, upper):
        column = lax.dynamic_slice_in_dim(upper, step, 1, 1)[:, 0]
        target = lax.dynamic_slice_in_dim(gram, step, 1, 0)[0]
        remain = target - jnp.dot(column, upper, precision=lax.Precision.HIGHEST)
        pivot = jnp.sqrt(lax.dynamic_slice_in_dim(remain, step, 1, 0)[0])
        new_row = jnp.where(columns >= step, remain / pivot, 0.0)
        return lax.dynamic_update_slice_in_dim(upper, new_row[None, :], step, 0)

    return lax.fori_loop(0, width, cholesky_one_row, jnp.zeros((width, width), jnp.float32))


def upper_inverse(upper):
    width = upper.shape[0]
    columns = jnp.arange(width, dtype=jnp.int32)

    def upper_one_row(count, inverse):
        step = width - 1 - count
        row_u = lax.dynamic_slice_in_dim(upper, step, 1, 0)[0]
        pivot = lax.dynamic_slice_in_dim(row_u, step, 1, 0)[0]
        unit_row = (columns == step).astype(jnp.float32)
        new_row = (unit_row - jnp.dot(row_u, inverse, precision=lax.Precision.HIGHEST)) / pivot
        return lax.dynamic_update_slice_in_dim(inverse, new_row[None, :], step, 0)

    return lax.fori_loop(0, width, upper_one_row, jnp.zeros((width, width), jnp.float32))


def slot_select(from_here, values, slot_count):
    own_count = from_here.shape[1]
    positions = jnp.arange(own_count, dtype=jnp.int32)
    before_mask = (positions[:, None] < positions[None, :]).astype(jnp.float32)
    slot_rank = jnp.dot(
        from_here.astype(jnp.float32), before_mask, precision=lax.Precision.HIGHEST
    ).astype(jnp.int32)
    slot_ids = jnp.arange(slot_count, dtype=jnp.int32)
    slot_hit = from_here[:, :, None] & (slot_rank[:, :, None] == slot_ids[None, None, :])
    picked = jnp.sum(jnp.where(slot_hit, values[:, :, None], 0), axis=1)
    slot_valid = jnp.any(slot_hit, axis=1).astype(jnp.float32)
    return (picked, slot_valid)


def rank_within(keys_mine):
    own_count = keys_mine.shape[0]
    positions = jnp.arange(own_count, dtype=jnp.int32)
    same_key = keys_mine[:, None] == keys_mine[None, :]
    earlier_rows = positions[None, :] < positions[:, None]
    return jnp.sum((same_key & earlier_rows).astype(jnp.int32), axis=1)


def per_device(features, sign_bits, sample_device, sample_offset):
    highest = lax.Precision.HIGHEST
    rows_dev, feat_width = features.shape
    n_outer = lax.axis_size("exa")
    n_inner = lax.axis_size("exb")
    n_all = n_outer * n_inner
    myself = lax.axis_index("exa") * n_inner + lax.axis_index("exb")
    sign_values = (2 * sign_bits - 1).astype(jnp.float32)
    signed = features * sign_values[:, None]
    blocks = rows_dev // 128
    local_grid = signed.reshape(blocks, 128, feat_width)
    local_grid = jnp.einsum("kj,bjf->bkf", hadamard_table(128), local_grid, precision=highest)
    local_grid = jnp.einsum("kb,bjf->kjf", hadamard_table(blocks), local_grid, precision=highest)
    signed_local = local_grid.reshape(rows_dev, feat_width)
    piece_rows = rows_dev // n_all
    all_table = hadamard_table(n_all)
    mixed = jnp.einsum(
        "ks,spf->kpf",
        all_table,
        lax.all_to_all(
            signed_local.reshape(n_all, piece_rows, feat_width),
            ("exa", "exb"),
            split_axis=0,
            concat_axis=0,
            tiled=True,
        ),
        precision=highest,
    )
    scale = 1.0 / math.sqrt(rows_dev * n_all)
    total_samples = sample_device.shape[0]
    own_count = total_samples // n_all
    source_all = sample_device[:, 0].reshape(n_all, own_count)
    offset_all = sample_offset.reshape(n_all, own_count)
    offset_mine = lax.dynamic_slice_in_dim(sample_offset, myself * own_count, own_count)
    group_rows = rows_dev // n_all
    group_slots = max(4, 2 * own_count // n_all)
    group_all = offset_all // group_rows
    within_all = offset_all % group_rows
    group_mine = offset_mine // group_rows
    flat_all = source_all * group_rows + within_all
    held_flat = mixed.reshape(n_all * group_rows, feat_width)
    from_here = group_all == myself
    picked_rows, slot_valid = slot_select(from_here, flat_all, group_slots)
    outgoing = jnp.take(held_flat, picked_rows.reshape(-1), axis=0) * (
        slot_valid.reshape(-1)[:, None] * scale
    )
    outgoing = outgoing.reshape(n_all, group_slots, feat_width)
    received = lax.all_to_all(outgoing, ("exa", "exb"), split_axis=0, concat_axis=0, tiled=True)
    rank_mine = rank_within(group_mine)
    sketch = jnp.take(
        received.reshape(n_all * group_slots, feat_width),
        group_mine * group_slots + rank_mine,
        axis=0,
    )
    gram_local = jnp.dot(sketch.T, sketch, precision=highest) / total_samples
    gram = over_pieces(gram_local, ("exa", "exb"))
    upper_factor = cholesky_upper(gram)
    inverse = upper_inverse(upper_factor)
    q_rows = jnp.dot(sketch, inverse, precision=highest)
    return (q_rows, upper_factor)


def solution(mesh):
    placed = (P(("exa", "exb"), None), P(("exa", "exb")), P(), P())
    return jax.shard_map(
        per_device,
        mesh=mesh,
        in_specs=placed,
        out_specs=(P(("exa", "exb"), None), P()),
        check_vma=False,
    )
```

profile of v0, /device:TPU:1, one launch (start us, length us, event | category | flops | bytes accessed | tf_op | source)
XLA Modules:
  0.0 661.0 jit_solution(1622086267628406629)
XLA Ops:
  7.9 5.0 broadcast_multiply_fusion
  12.9 8.3 %convolution_bitcast_fusion.2 = f32[64,128,128]{1,2,0:T(8,128)} fusion(f32[64,128,128]{2,1,0:T(8,128)S(1)} %bitcast.72), kind=kOutput, calls=%fused_computation.20 | convolution fusion | flops 1611235328 | bytes 8388608 | tf_op jit(solution)/shard_map/kj,bjf->bkf/dot_general | solution.py:86
  21.2 5.4 copy.28
  26.6 5.5 fusion.43
  32.1 4.4 copy.29
  36.5 12.0 %all-to-all-start = ((f32[128,64,128]{2,1,0:T(8,128)}), f32[128,64,128]{2,1,0:T(8,128)}, u32[]{:S(2)}, u32[]{:S(2)}) async-start(f32[128,64,128]{2,1,0:T(8,128)} %bitcast.70), calls=%async_computation | async-start | bytes 8388608 | tf_op jit(solution)/shard_map/all_to_all | solution.py:94
  50.0 2.2 select_reduce_fusion
  52.3 2.3 fusion.17
  54.7 46.2 %all-to-all-done = f32[128,64,128]{2,1,0:T(8,128)} async-done(((f32[128,64,128]{2,1,0:T(8,128)}), f32[128,64,128]{2,1,0:T(8,128)}, u32[]{:S(2)}, u32[]{:S(2)}) %all-to-all-start) | async-done | bytes 4194336 | tf_op jit(solution)/shard_map/all_to_all | solution.py:94
  100.8 8.3 %fusion.14 = f32[128,64,128]{2,0,1:T(8,128)S(1)} fusion(f32[128,64,128]{2,1,0:T(8,128)} %all-to-all-done), kind=kOutput, calls=%fused_computation.18 | convolution fusion | flops 1611235328 | bytes 8388608 | tf_op jit(solution)/shard_map/ks,spf->kpf/dot_general | solution.py:91
  109.2 4.4 copy.31
  113.5 5.2 gather_fusion
  118.7 1.1 fusion.19
  119.9 4.2 all-to-all-start.1
  124.6 12.8 %all-to-all-done.1 = f32[128,8,128]{2,1,0:T(8,128)S(1)} async-done(((f32[128,8,128]{2,1,0:T(8,128)}), f32[128,8,128]{2,1,0:T(8,128)S(1)}, u32[]{:S(2)}, u32[]{:S(2)}) %all-to-all-start.1) | async-done | bytes 524320 | tf_op jit(solution)/shard_map/all_to_all | solution.py:122
  137.4 1.0 gather_fusion.1
  138.4 1.4 convolution_multiply_fusion
  139.9 66.6 %all-gather.3.cloned.1.call-done = f32[16384,128]{1,0:T(8,128)} async-done(((f32[128,128]{1,0:T(8,128)}), f32[16384,128]{1,0:T(8,128)}) %all-gather.3.cloned.1.call-update) | async-done | bytes 8388624 | tf_op jit(solution)/shard_map/all_gather | solution.py:10
  206.5 3.8 reduce_sum.29
  210.3 257.4 %while.31 = (s32[]{:T(128)}, f32[128,128]{0,1:T(8,128)S(1)}, f32[128,128]{1,0:T(8,128)S(1)}, s32[]{:T(128)}, s32[]{:T(128)}) while((s32[]{:T(128)}, f32[128,128]{0,1:T(8,128)S(1)}, f32[128,128]{1,0:T(8,128)S(1)}, s32[]{:T(128)}, s32[]{:T(128)}) %tuple.85), condition=%wide.region_5.6_spmd.clone, body=%wide.region_4.5_spmd.clone.sunk | while | flops 197122 | bytes 71261 | solution.py:35
  467.8 185.3 %while.32 = (s32[]{:T(128)}, f32[128,128]{1,0:T(8,128)S(1)}, f32[128,128]{1,0:T(8,128)S(1)}, s32[]{:T(128)}, s32[]{:T(128)}, /*index=5*/s32[]{:T(128)}, s32[]{:T(128)}) while((s32[]{:T(128)}, f32[128,128]{1,0:T(8,128)S(1)}, f32[128,128]{1,0:T(8,128)S(1)}, s32[]{:T(128)}, s32[]{:T(128)}, /*index=5*/s32[]{:T(128)}, s32[]{:T(128)}) %tuple.88), condition=%wide.region_7.8_spmd.clone, body=%wide.region_6.7_spmd.clone.sunk | while | flops 197127 | bytes 67751 | solution.py:50
  474.2 0.8 fusion.117
  491.6 0.8 fusion.117
  653.1 1.1 fusion.23
  (1049 shorter events, 347.3 us)
Async XLA Ops:
  36.5 12.0 %copy-start = (s32[65536]{0:T(1024)S(1)}, s32[65536]{0:T(1024)}, u32[]{:S(2)}) copy-start(s32[65536]{0:T(1024)} %param.11) | copy-start | bytes 786436
  36.5 12.0 %copy-start.1 = (s32[65536,1]{0,1:T(1,128)S(1)}, s32[65536,1]{0,1:T(1,128)}, u32[]{:S(2)}) copy-start(s32[65536,1]{0,1:T(1,128)} %param.10) | copy-start | bytes 786436
  36.5 64.3 %all-to-all-start = ((f32[128,64,128]{2,1,0:T(8,128)}), f32[128,64,128]{2,1,0:T(8,128)}, u32[]{:S(2)}, u32[]{:S(2)}) async-start(f32[128,64,128]{2,1,0:T(8,128)} %bitcast.70), calls=%async_computation | async-start | bytes 8388608 | tf_op jit(solution)/shard_map/all_to_all | solution.py:94
  119.9 17.5 %all-to-all-start.1 = ((f32[128,8,128]{2,1,0:T(8,128)}), f32[128,8,128]{2,1,0:T(8,128)S(1)}, u32[]{:S(2)}, u32[]{:S(2)}) async-start(f32[128,8,128]{2,1,0:T(8,128)} %fusion.19), calls=%async_computation.1 | async-start | bytes 1048576 | tf_op jit(solution)/shard_map/all_to_all | solution.py:122
  124.1 82.4 %all-gather.3.cloned.1.call-start = ((), (), s32[]{:S(2)}) async-start(), calls=%async_computation.2 | async-start | bytes 8454144 | tf_op jit(solution)/shard_map/all_gather | solution.py:10
  653.1 1.1 copy-start.2
Sparse Core Ops, SparseCore 0:
  140.0 66.4 all-gather.2
where the time goes:
time: 664 us; the launch traced here: 661 us
  local copies, waits for them, and re-layouts  242 us (36%)
  matrix products  149 us (22%)
  waiting for transfers between devices  126 us (19%)
  loops' own time  96.7 us (15%)
  other arithmetic  17.4 us (3%)
  starting transfers between devices  16.2 us (2%)
  between operations  14.3 us (2%)
    dot_general x128, matrix products, upper_one_row(): jnp.dot(row_u, inverse, precision=lax.Precision.HIGHEST)  102 us
    another operation x1, loops' own time, cholesky_upper(): lax.fori_loop(0, width, cholesky_one_row, jnp.zeros((width, width), jnp.f...  92.7 us
    dynamic_slice x128, local copies, waits for them, and re-layouts, cholesky_one_row(): pivot = jnp.sqrt(lax.dynamic_slice_in_dim(remain, step, 1, 0)[0])  81.4 us
    dynamic_slice x128, local copies, waits for them, and re-layouts, upper_one_row(): pivot = lax.dynamic_slice_in_dim(row_u, step, 1, 0)[0]  75.3 us
    all_gather x1, waiting for transfers between devices, over_pieces(): blocks = lax.all_gather(x, axis)  66.6 us
    all_to_all x1, waiting for transfers between devices, per_device(): lax.all_to_all(signed_local.reshape(n_all, piece_rows, feat_width), ('exa...  46.2 us
    dynamic_update_slice x128, local copies, waits for them, and re-layouts, cholesky_one_row(): return lax.dynamic_update_slice_in_dim(upper, new_row[None, :], step, 0)  45.9 us
    dot_general x128, matrix products, cholesky_one_row(): remain = target - jnp.dot(column, upper, precision=lax.Precision.HIGHEST)  22.1 us
  transfers between devices with their start and end apart: 3, of which 3 were waited for; matrix products, arithmetic and copies ran while one was open for 1% of the time, Pallas kernels for 0%

commit v1 on v0

--- a/solution.py
+++ b/solution.py
@@ -3,12 +3,9 @@
 import jax
 import jax.numpy as jnp
 from jax import lax
+from jax.experimental import pallas as pl
+from jax.experimental.pallas import tpu as pltpu
 from jax.sharding import PartitionSpec as P
-
-
-def over_pieces(x, axis):
-    blocks = lax.all_gather(x, axis)
-    return blocks.sum(axis=0)
 
 
 def hadamard_table(order_size):
@@ -20,34 +17,55 @@
     return (1 - 2 * (parity % 2)).astype(jnp.float32)
 
 
-def cholesky_upper(gram):
-    width = gram.shape[0]
-    columns = jnp.arange(width, dtype=jnp.int32)
-
-    def cholesky_one_row(step, upper):
-        column = lax.dynamic_slice_in_dim(upper, step, 1, 1)[:, 0]
-        target = lax.dynamic_slice_in_dim(gram, step, 1, 0)[0]
-        remain = target - jnp.dot(column, upper, precision=lax.Precision.HIGHEST)
-        pivot = jnp.sqrt(lax.dynamic_slice_in_dim(remain, step, 1, 0)[0])
-        new_row = jnp.where(columns >= step, remain / pivot, 0.0)
-        return lax.dynamic_update_slice_in_dim(upper, new_row[None, :], step, 0)
-
-    return lax.fori_loop(0, width, cholesky_one_row, jnp.zeros((width, width), jnp.float32))
+def factor(gram_ref, upper_ref, inverse_ref, work):
+    width = 128
+    rows = lax.broadcasted_iota(jnp.int32, (8, width), 0)
+    lanes = lax.broadcasted_iota(jnp.int32, (8, width), 1)
+    work[:, :width] = gram_ref[...]
+    work[:, width:] = (
+        lax.broadcasted_iota(jnp.int32, (width, width), 0)
+        == lax.broadcasted_iota(jnp.int32, (width, width), 1)
+    ).astype(jnp.float32)
+    for panel in range(width // 8):
+        low = 8 * panel
+        left = work[low : low + 8, :width]
+        right = work[low : low + 8, width:]
+        cols = [
+            jnp.broadcast_to(left[:, low + j : low + j + 1], (8, width)) for j in range(8)
+        ]
+        pivots = jnp.ones((8, width), jnp.float32)
+        for i in range(8):
+            pivot = jnp.broadcast_to(cols[i][i : i + 1, :], (8, width))
+            pivots = jnp.where(rows == i, pivot, pivots)
+            if i < 7:
+                scaled = jnp.where(rows > i, cols[i] / pivot, 0.0)
+                for j in range(i + 1, 8):
+                    cols[j] = cols[j] - scaled * cols[j][i : i + 1, :]
+                left = left - scaled * left[i : i + 1, :]
+                right = right - scaled * right[i : i + 1, :]
+        root = lax.rsqrt(pivots)
+        root = root * (1.5 - 0.5 * pivots * root * root)
+        left = jnp.where(lanes >= rows + low, left * root, 0.0)
+        right = right * root
+        upper_ref[low : low + 8, :] = left
+        inverse_ref[low : low + 8, :] = right
+        if low + 8 < width:
+            change = lax.dot_general(
+                left,
+                jnp.concatenate([left, right], axis=1),
+                (((0,), (0,)), ((), ())),
+                precision=lax.Precision.HIGHEST,
+                preferred_element_type=jnp.float32,
+            )
+            work[low + 8 :, :] = work[low + 8 :, :] - change[low + 8 :, :]
 
 
-def upper_inverse(upper):
-    width = upper.shape[0]
-    columns = jnp.arange(width, dtype=jnp.int32)
-
-    def upper_one_row(count, inverse):
-        step = width - 1 - count
-        row_u = lax.dynamic_slice_in_dim(upper, step, 1, 0)[0]
-        pivot = lax.dynamic_slice_in_dim(row_u, step, 1, 0)[0]
-        unit_row = (columns == step).astype(jnp.float32)
-        new_row = (unit_row - jnp.dot(row_u, inverse, precision=lax.Precision.HIGHEST)) / pivot
-        return lax.dynamic_update_slice_in_dim(inverse, new_row[None, :], step, 0)
-
-    return lax.fori_loop(0, width, upper_one_row, jnp.zeros((width, width), jnp.float32))
+def factor_call(gram):
+    return pl.pallas_call(
+        factor,
+        out_shape=[jax.ShapeDtypeStruct((128, 128), jnp.float32)] * 2,
+        scratch_shapes=[pltpu.VMEM((128, 256), jnp.float32)],
+    )(gram)
 
 
 def slot_select(from_here, values, slot_count):
@@ -127,10 +145,9 @@
         axis=0,
     )
     gram_local = jnp.dot(sketch.T, sketch, precision=highest) / total_samples
-    gram = over_pieces(gram_local, ("exa", "exb"))
-    upper_factor = cholesky_upper(gram)
-    inverse = upper_inverse(upper_factor)
-    q_rows = jnp.dot(sketch, inverse, precision=highest)
+    gram = lax.psum(gram_local, ("exa", "exb"))
+    upper_factor, inverse = factor_call(gram)
+    q_rows = jnp.dot(sketch, inverse.T, precision=highest)
     return (q_rows, upper_factor)
 
 

time: 664 us -> 295 us (0.44)
  local copies, waits for them, and re-layouts: 242 us -> 20.6 us
  matrix products: 149 us -> 25.8 us
  loops' own time: 96.7 us -> 0 us
  waiting for transfers between devices: 126 us -> 195 us
  Pallas kernels: 0 us -> 10 us
    dynamic_slice x256 -> x0, local copies, waits for them, and re-layouts: 157 us -> none  [the longest x128 81.4 us: cholesky_one_row(): pivot = jnp.sqrt(lax.dynamic_slice_in_dim(remain, step, 1, 0)[0])]
    psum x0 -> x1, waiting for transfers between devices: none -> 136 us  [per_device(): gram = lax.psum(gram_local, ('exa', 'exb'))]
    dot_general x257 -> x1, matrix products: 125 us -> 1.97 us  [per_device(): q_rows = jnp.dot(sketch, inverse.T, precision=highest)]
    another operation x2 -> x0, loops' own time: 96.7 us -> none  [the longest x1 92.7 us: cholesky_upper(): lax.fori_loop(0, width, cholesky_one_row, jnp.zeros((width, width), jnp.f...]
    all_gather x1 -> x0, waiting for transfers between devices: 66.6 us -> none  [over_pieces(): blocks = lax.all_gather(x, axis)]
    dynamic_update_slice x256 -> x0, local copies, waits for them, and re-layouts: 49.9 us -> none  [the longest x128 45.9 us: cholesky_one_row(): return lax.dynamic_update_slice_in_dim(upper, new_row[None, :], step, 0)]
    broadcast_in_dim x128 -> x0, local copies, waits for them, and re-layouts: 14.5 us -> none  [cholesky_one_row(): return lax.dynamic_update_slice_in_dim(upper, new_row[None, :], step, 0)]
    pallas_call x0 -> x1, Pallas kernels: none -> 10 us  [factor_call(): pl.pallas_call(factor, out_shape=[jax.ShapeDtypeStruct((128, 128), jnp.fl...]
  transfers between devices with their start and end apart: 3 -> 3, of which waited for: 3 -> 3; matrix products, arithmetic and copies ran while one was open for 1% -> 2% of each run, Pallas kernels for 0% -> 0%
where the time goes in v1:
time: 295 us
  waiting for transfers between devices  195 us (66%)
  matrix products  25.8 us (9%)
  local copies, waits for them, and re-layouts  20.6 us (7%)
  starting transfers between devices  16.2 us (5%)
  between operations  14.2 us (5%)
  other arithmetic  12.9 us (4%)
  Pallas kernels  10 us (3%)
    psum x1, waiting for transfers between devices, per_device(): gram = lax.psum(gram_local, ('exa', 'exb'))  136 us
    all_to_all x1, waiting for transfers between devices, per_device(): lax.all_to_all(signed_local.reshape(n_all, piece_rows, feat_width), ('exa...  46.2 us
    all_to_all x1, waiting for transfers between devices, per_device(): lax.all_to_all(outgoing, ('exa', 'exb'), split_axis=0, concat_axis=0, til...  12.8 us
    all_to_all x1, starting transfers between devices, per_device(): lax.all_to_all(signed_local.reshape(n_all, piece_rows, feat_width), ('exa...  12 us
    pallas_call x1, Pallas kernels, factor_call(): pl.pallas_call(factor, out_shape=[jax.ShapeDtypeStruct((128, 128), jnp.fl...  10 us
    dot_general x1, matrix products, per_device(): jnp.einsum('kj,bjf->bkf', hadamard_table(128), local_grid, precision=high...  8.34 us
    dot_general x1, matrix products, per_device(): jnp.einsum('ks,spf->kpf', all_table, lax.all_to_all(signed_local.reshape(...  8.32 us
  transfers between devices with their start and end apart: 3, of which 3 were waited for; matrix products, arithmetic and copies ran while one was open for 2% of the time, Pallas kernels for 0%

profile of v1, /device:TPU:1, one launch (start us, length us, event | category | flops | bytes accessed | tf_op | source)
XLA Modules:
  0.0 295.0 jit_solution(10500154140679569098)
XLA Ops:
  7.2 0.8 add_convert_fusion
  7.9 5.0 %broadcast_multiply_fusion = f32[8192,128]{1,0:T(8,128)S(1)} fusion(f32[8192,128]{1,0:T(8,128)} %param.4, f32[8192]{0:T(1024)S(1)} %add_convert_fusion), kind=kLoop, calls=%fused_computation.5 | loop fusion | flops 1048576 | bytes 8421376 | tf_op jit(solution)/shard_map/mul | solution.py:101
  12.9 8.3 %convolution_bitcast_fusion = f32[64,128,128]{1,2,0:T(8,128)} fusion(f32[64,128,128]{2,1,0:T(8,128)S(1)} %bitcast.24), kind=kOutput, calls=%fused_computation.4 | convolution fusion | flops 1611235328 | bytes 8388608 | tf_op jit(solution)/shard_map/kj,bjf->bkf/dot_general | solution.py:104
  21.2 5.4 %copy.15 = f32[64,128,128]{2,0,1:T(8,128)} copy(f32[64,128,128]{1,2,0:T(8,128)} %convolution_bitcast_fusion) | data formatting | bytes 8388608 | tf_op jit(solution)/shard_map/kj,bjf->bkf/transpose | solution.py:104
  26.6 5.5 %fusion.29 = f32[64,128,128]{2,0,1:T(8,128)S(1)} fusion(f32[64,128,128]{2,0,1:T(8,128)} %copy.15), kind=kOutput, calls=%fused_computation.54 | convolution fusion | flops 805449728 | bytes 8388608 | tf_op jit(solution)/shard_map/kb,bjf->kjf/dot_general | solution.py:105
  32.1 4.4 %copy.16 = f32[64,128,128]{2,1,0:T(8,128)} copy(f32[64,128,128]{2,0,1:T(8,128)S(1)} %fusion.29) | data formatting | bytes 8388608 | tf_op jit(solution)/shard_map/kb,bjf->kjf/dot_general | solution.py:105
  36.5 12.0 %all-to-all-start = ((f32[128,64,128]{2,1,0:T(8,128)}), f32[128,64,128]{2,1,0:T(8,128)}, u32[]{:S(2)}, u32[]{:S(2)}) async-start(f32[128,64,128]{2,1,0:T(8,128)} %bitcast.22), calls=%async_computation | async-start | bytes 8388608 | tf_op jit(solution)/shard_map/all_to_all | solution.py:112
  48.5 0.7 multiply_reduce_fusion
  49.6 0.2 convolution_convert_fusion
  50.0 2.2 select_reduce_fusion
  52.3 2.3 fusion.3
  54.7 46.2 %all-to-all-done = f32[128,64,128]{2,1,0:T(8,128)} async-done(((f32[128,64,128]{2,1,0:T(8,128)}), f32[128,64,128]{2,1,0:T(8,128)}, u32[]{:S(2)}, u32[]{:S(2)}) %all-to-all-start) | async-done | bytes 4194336 | tf_op jit(solution)/shard_map/all_to_all | solution.py:112
  100.8 8.3 %fusion = f32[128,64,128]{2,0,1:T(8,128)S(1)} fusion(f32[128,64,128]{2,1,0:T(8,128)} %all-to-all-done), kind=kOutput, calls=%fused_computation.2 | convolution fusion | flops 1611235328 | bytes 8388608 | tf_op jit(solution)/shard_map/ks,spf->kpf/dot_general | solution.py:109
  109.2 4.4 %copy.18 = f32[128,64,128]{2,1,0:T(8,128)} copy(f32[128,64,128]{2,0,1:T(8,128)S(1)} %fusion) | data formatting | bytes 8388608 | tf_op jit(solution)/shard_map/ks,spf->kpf/dot_general | solution.py:109
  113.5 5.2 %gather_fusion = f32[1024,128]{1,0:T(8,128)S(1)} fusion(f32[8192,128]{1,0:T(8,128)} %bitcast.23, s32[1024]{0:T(1024)S(1)} %broadcast_clamp_fusion), kind=kCustom, calls=%fused_computation | custom fusion | bytes 1052672 | tf_op jit(solution)/shard_map/jit(_take)/gather | solution.py:136
  118.7 1.1 fusion.5
  119.9 4.2 %all-to-all-start.1 = ((f32[128,8,128]{2,1,0:T(8,128)}), f32[128,8,128]{2,1,0:T(8,128)S(1)}, u32[]{:S(2)}, u32[]{:S(2)}) async-start(f32[128,8,128]{2,1,0:T(8,128)} %fusion.5), calls=%async_computation.1 | async-start | bytes 1048576 | tf_op jit(solution)/shard_map/all_to_all | solution.py:140
  124.2 0.3 convert_reduce_fusion
  124.6 12.8 %all-to-all-done.1 = f32[128,8,128]{2,1,0:T(8,128)S(1)} async-done(((f32[128,8,128]{2,1,0:T(8,128)}), f32[128,8,128]{2,1,0:T(8,128)S(1)}, u32[]{:S(2)}, u32[]{:S(2)}) %all-to-all-start.1) | async-done | bytes 524320 | tf_op jit(solution)/shard_map/all_to_all | solution.py:140
  137.4 1.0 gather_fusion.1
  138.4 1.4 convolution_multiply_fusion
  139.9 136.3 %all-reduce.2.cloned.1.call-done.gram_ref = f32[128,128]{1,0:T(8,128)} async-done(((f32[128,128]{1,0:T(8,128)}), f32[128,128]{1,0:T(8,128)}) %all-reduce.2.cloned.1.call-update) | async-done | bytes 65552 | tf_op jit(solution)/shard_map/psum | solution.py:148
  276.1 10.0 %shard_map.59 = (f32[128,128]{1,0:T(8,128)}, f32[128,128]{1,0:T(8,128)}) custom-call(f32[128,128]{1,0:T(8,128)} %all-reduce.2.cloned.1.call-done.gram_ref), custom_call_target="tpu_custom_call" | custom-call | tf_op jit(solution)/shard_map/pallas_call | solution.py:64
  286.1 2.0 fusion.9
  (18 shorter events, 0.8 us)
Async XLA Ops:
  36.5 12.0 %copy-start.1 = (s32[65536,1]{0,1:T(1,128)S(1)}, s32[65536,1]{0,1:T(1,128)}, u32[]{:S(2)}) copy-start(s32[65536,1]{0,1:T(1,128)} %param.6) | copy-start | bytes 786436
  36.5 12.8 %copy-start = (s32[65536]{0:T(1024)S(1)}, s32[65536]{0:T(1024)}, u32[]{:S(2)}) copy-start(s32[65536]{0:T(1024)} %param.7) | copy-start | bytes 786436
  36.5 64.3 %all-to-all-start = ((f32[128,64,128]{2,1,0:T(8,128)}), f32[128,64,128]{2,1,0:T(8,128)}, u32[]{:S(2)}, u32[]{:S(2)}) async-start(f32[128,64,128]{2,1,0:T(8,128)} %bitcast.22), calls=%async_computation | async-start | bytes 8388608 | tf_op jit(solution)/shard_map/all_to_all | solution.py:112
  119.9 17.5 %all-to-all-start.1 = ((f32[128,8,128]{2,1,0:T(8,128)}), f32[128,8,128]{2,1,0:T(8,128)S(1)}, u32[]{:S(2)}, u32[]{:S(2)}) async-start(f32[128,8,128]{2,1,0:T(8,128)} %fusion.5), calls=%async_computation.1 | async-start | bytes 1048576 | tf_op jit(solution)/shard_map/all_to_all | solution.py:140
  124.1 152.0 %all-reduce.2.cloned.1.call-start = ((), (), s32[]{:S(2)}) async-start(), calls=%async_computation.2 | async-start | bytes 131072 | tf_op jit(solution)/shard_map/psum | solution.py:148
Sparse Core Ops, SparseCore 0:
  140.0 136.0 all-reduce.1
